TPU v7x, 128 devices: a whole 4x4x4 slice. The times are simulated.
128 devices in a mesh: row: 8 (over x, core), col: 16 (over z, y).
Axes of the slice: x: 4, y: 4, z: 4, core: 2. Of those that a mesh axis runs over, the one named last changes fastest.
Arguments:
- send_cells: int32 [128, 128, 512], P(('row', 'col')), may hold values from 0 to 65535, as said below
- send_species: int32 [128, 128, 512], P(('row', 'col')), may hold values from 0 to 5
- send_mix: bfloat16 [128, 6, 128, 512], P(('row', 'col')), may hold values from 0 to 0.5
- send_counts: int32 [128, 128], P(('row', 'col')), may hold values from 64 to 512, as said below
- chi: float32 [6, 6], replicated, may hold values from 0 to 8
Outputs:
- forces: float32 [128, 3, 128, 512], P(('row', 'col'))
Inputs may be any that keep to these rules, and one draw needn't show every extreme that they name: `send_cells`: local cell (x * 16 + y) * 256 + z in the destination brick; domain s (flat index) holds particles with z from s * 2 to (s + 1) * 2 - 1 only. `send_counts`: slots at or beyond the count are unused. At most 512 particles go from one domain to one brick; in every draw some domain fills a slot list, and one brick receives 512 from every domain.
All inputs are finite; a program needn't handle non-finite values.
Results may differ from a plain program's by a relative error of at most 0.0023.
Values may be sent and summed in bfloat16 or wider, within the bound.
No kernel may reach another device: no remote copies, remote signals or barrier semaphores. Data moves between devices by JAX's collectives and lax.ppermute only.
A program may use at most 256 MiB of HBM per device.

v0:
```python
import functools

import jax
import jax.numpy as jnp
import numpy as np
from jax import lax
from jax.experimental import pallas as pl
from jax.experimental.pallas import tpu as pltpu
from jax.sharding import PartitionSpec as P


SPECIES = 6
ROWS = 8
COLS = 16
HALVES = 16
LANES = 128
SLOTS = 512
GROUP = 8
WIDE = COLS + 1
SLOT = GROUP + 1
MIB = 1 << 20
LIMIT = 60

raw_taps = (0.1353352832366127, 0.6065306597126334, 1.0)
tap_total = raw_taps[2] + 2.0 * (raw_taps[0] + raw_taps[1])
T2, T1, T0 = (t / tap_total for t in raw_taps)

f32 = jnp.float32
bf16 = jnp.bfloat16


def digits_of(row):
    wide = jnp.broadcast_to(row, (8, SLOTS))
    low = (wide >> 8) & 15
    ids = lax.broadcasted_iota(jnp.int32, (8, SLOTS), 0)
    inner = jnp.concatenate(
        [jnp.where(low == ids, 1.0, 0.0), jnp.where(low == ids + 8, 1.0, 0.0)], axis=0
    ).astype(bf16)
    high = (wide >> 12).astype(f32)
    return inner, jnp.concatenate([high, high], axis=0).astype(bf16)


def table_of(inner, outer, count):
    none = jnp.zeros((16, SLOTS), bf16)
    return jnp.concatenate(
        [jnp.where(outer == jnp.full((16, SLOTS), i, bf16), inner, none) for i in range(count)], axis=0
    )


def weights_of(limit, t, rows, species, mix):
    part = pl.ds(t * LANES, LANES)
    lane = lax.broadcasted_iota(jnp.int32, (COLS, LANES), 1)
    valid = (lane + t * LANES) < limit
    kind = species[rows, part]
    found = []
    for k in range(SPECIES):
        w = jnp.where(kind == k, 1.0, 0.0) + mix[k, rows, part].astype(f32)
        found.append(jnp.where(valid, w, 0.0).astype(bf16).astype(f32))
    return found


def limits_of(counts, first):
    rows = lax.broadcasted_iota(jnp.int32, (COLS, LANES), 0)
    limit = jnp.zeros((COLS, LANES), jnp.int32)
    for i in range(COLS):
        limit = jnp.where(rows == i, counts[first + i], limit)
    return limit


def deposit_kernel(counts_far, cells_far, species_far, mix_far, own_far, first_far, second_far,
                   counts, cells, species, mix, own, first_s, second_s, w_s, d_s, sems, out_sems, count_sem):
    even = jnp.full((COLS, LANES), lax.axis_index("col") % 2, jnp.int32) == 0

    def fetches(r):
        rows = pl.ds(pl.multiple_of(r * COLS, COLS), COLS)
        return (
            pltpu.make_async_copy(cells_far.at[rows], cells.at[rows], sems.at[0, r]),
            pltpu.make_async_copy(species_far.at[rows], species.at[rows], sems.at[1, r]),
            pltpu.make_async_copy(mix_far.at[:, rows], mix.at[:, rows], sems.at[2, r]),
        )

    def results(r):
        part = pl.ds(2 * r, 2)
        return [
            pltpu.make_async_copy(near.at[:, part] if i < 2 else near.at[:, :, part],
                                  far.at[:, part] if i < 2 else far.at[:, :, part], out_sems.at[i, r])
            for i, (near, far) in enumerate(((first_s, first_far), (second_s, second_far), (own, own_far)))
        ]

    count_copy = pltpu.make_async_copy(counts_far, counts, count_sem)
    count_copy.start()
    for r in range(ROWS):
        for copy in fetches(r):
            copy.start()
    zero = jnp.zeros((COLS, LANES), f32)
    for t in range(4):
        for k in (6, 7):
            w_s[t, k * WIDE:k * WIDE + COLS] = zero
            w_s[t, (8 + k) * WIDE:(8 + k) * WIDE + COLS] = zero

    count_copy.wait()

    def one_row(r, carry):
        for copy in fetches(r):
            copy.wait()
        first = pl.multiple_of(r * COLS, COLS)
        rows = pl.ds(first, COLS)
        limit = limits_of(counts, first)
        for t in range(4):
            upper = (cells[rows, pl.ds(t * LANES, LANES)] & 1) == 1
            for k, w in enumerate(weights_of(limit, t, rows, species, mix)):
                w_s[t, k * WIDE:k * WIDE + COLS] = jnp.where(upper, 0.0, w)
                w_s[t, (8 + k) * WIDE:(8 + k) * WIDE + COLS] = jnp.where(upper, w, 0.0)
        for b in range(COLS):
            inner, outer = digits_of(cells[pl.ds(first + b, 1), :])
            second = outer > 7.5
            table = table_of(inner, jnp.where(second, outer - 8.0, outer), 8)
            w = jnp.concatenate([w_s[t, pl.ds(b, 16, stride=WIDE)] for t in range(4)], axis=1).astype(bf16)
            none = jnp.zeros((16, SLOTS), bf16)
            halves = jnp.concatenate([jnp.where(second, none, w), jnp.where(second, w, none)], axis=0)
            dens = lax.dot_general(halves, table, (((1,), (1,)), ((), ())), preferred_element_type=f32)
            d_s[0, pl.ds(b, 16, stride=WIDE)] = dens[:16]
            d_s[1, pl.ds(b, 16, stride=WIDE)] = dens[16:]
        for k in range(SPECIES):
            for h in range(2):
                low, high = (d_s[h, (z * 8 + k) * WIDE:(z * 8 + k) * WIDE + COLS] for z in range(2))
                own[0, k, 2 * r + h] = low
                own[1, k, 2 * r + h] = high
                first_s[k, 2 * r + h] = jnp.where(even, high, low).astype(bf16)
                second_s[k, 2 * r + h] = jnp.where(even, low, high).astype(bf16)
        for copy in results(r):
            copy.start()
        return carry

    lax.fori_loop(0, ROWS, one_row, 0)
    for r in range(ROWS):
        for copy in results(r):
            copy.wait()


VM = pltpu.MemorySpace.VMEM
SM = pltpu.MemorySpace.SMEM
FAR = pltpu.MemorySpace.HBM


def deposit(counts, cells, species, mix):
    half = (HALVES, COLS, LANES)
    return pl.pallas_call(
        deposit_kernel,
        name="deposit",
        in_specs=[pl.BlockSpec(memory_space=FAR)] * 4,
        out_specs=[pl.BlockSpec(memory_space=FAR)] * 3,
        scratch_shapes=[
            pltpu.SMEM((ROWS * COLS,), jnp.int32),
            pltpu.VMEM((ROWS * COLS, SLOTS), jnp.int32),
            pltpu.VMEM((ROWS * COLS, SLOTS), jnp.int32),
            pltpu.VMEM((SPECIES, ROWS * COLS, SLOTS), bf16),
            pltpu.VMEM((2, SPECIES) + half, f32),
            pltpu.VMEM((SPECIES,) + half, bf16),
            pltpu.VMEM((SPECIES,) + half, bf16),
            pltpu.VMEM((4, 16 * WIDE, LANES), f32),
            pltpu.VMEM((2, 16 * WIDE, LANES), f32),
            pltpu.SemaphoreType.DMA((3, ROWS)),
            pltpu.SemaphoreType.DMA((3, ROWS)),
            pltpu.SemaphoreType.DMA,
        ],
        out_shape=[jax.ShapeDtypeStruct((2, SPECIES) + half, f32)]
        + [jax.ShapeDtypeStruct((SPECIES,) + half, bf16)] * 2,
        compiler_params=pltpu.CompilerParams(vmem_limit_bytes=LIMIT * MIB),
        cost_estimate=pl.CostEstimate(flops=10**9, bytes_accessed=5 * 10**6, transcendentals=0),
    )(*(pltpu.with_memory_space_constraint(v, FAR) for v in (counts, cells, species, mix)))


def mixing_kernel(counts, mix_matrix, species, mix, mixed):
    def one_row(r, carry):
        first = pl.multiple_of(r * COLS, COLS)
        rows = pl.ds(first, COLS)
        limit = limits_of(counts, first)
        for t in range(4):
            ws = weights_of(limit, t, rows, species, mix)
            for l in range(SPECIES):
                v = mix_matrix[l, 0] * ws[0]
                for k in range(1, SPECIES):
                    v = v + mix_matrix[l, k] * ws[k]
                mixed[l, rows, t * LANES:(t + 1) * LANES] = v
        return carry

    lax.fori_loop(0, ROWS, one_row, 0)


def mixing(counts, mix_matrix, species, mix):
    return pl.pallas_call(
        mixing_kernel,
        name="mixing",
        in_specs=[pl.BlockSpec(memory_space=SM)] * 2 + [pl.BlockSpec(memory_space=VM)] * 2,
        out_specs=pl.BlockSpec(memory_space=VM),
        out_shape=jax.ShapeDtypeStruct((SPECIES, ROWS * COLS, SLOTS), f32),
        compiler_params=pltpu.CompilerParams(vmem_limit_bytes=12 * MIB),
        cost_estimate=pl.CostEstimate(flops=10**9, bytes_accessed=4 * 10**6, transcendentals=0),
    )(counts, mix_matrix, species, mix)


def scaled_taps():
    smooth_scale, slope_scale = 1.6396387, 1.5596421
    smooth_taps = {0: T0, 1: T1, -1: T1, 2: T2, -2: T2}
    slope_taps = {1: 0.5 * (T0 - T2), 2: 0.5 * T1, 3: 0.5 * T2}
    slope_taps.update({-j: -v for j, v in slope_taps.items()})
    return (
        {j: smooth_scale * v for j, v in smooth_taps.items()},
        {j: slope_scale * v for j, v in slope_taps.items()},
        smooth_scale,
        slope_scale,
    )


SMOOTH, SLOPE, SMOOTH_SCALE, SLOPE_SCALE = scaled_taps()


def tap_matrices():
    lane = np.arange(LANES)
    x, y = lane // 16, lane % 16
    results = []
    for main, other, extent in ((y, x, 16), (x, y, 8)):
        source = np.concatenate([main, np.where(main < extent // 2, main + extent, main - extent)])
        same = np.concatenate([other, other])[:, None] == other[None, :]
        gap = source[:, None] - main[None, :]
        for taps in (SMOOTH, SLOPE):
            matrix = np.zeros((2 * LANES, LANES), np.float32)
            for j, value in taps.items():
                matrix += np.where(same & (gap == j), np.float32(value), np.float32(0))
            results.append(matrix)
    return jnp.asarray(np.concatenate(results, axis=1)).astype(bf16)


def split(v):
    top = v.astype(bf16)
    return top, (v - top.astype(f32)).astype(bf16)


def smooth_kernel(planes, even_ref, taps, *refs):
    flat = planes == FLAT
    if flat:
        own, first_a, first_b, second_a, second_b, ready, partial, x_s, y_s, w_s, g_s = refs
    else:
        partial, far_a, far_b, ready, x_s, y_s, w_s, g_s = refs
    outs = (0, 1, 2, 3) if flat else (4, 5)
    rows_of, count = ROWS_OF[planes]
    k = pl.program_id(0)
    lane = lax.broadcasted_iota(jnp.int32, (COLS, LANES), 1)
    col = lane & 15
    lower = lane.astype(f32).astype(bf16) < 64
    cu = 1.0 / (SMOOTH_SCALE * SLOPE_SCALE)
    cz = 0.5 / (SMOOTH_SCALE * SMOOTH_SCALE)
    even = jnp.full((COLS, LANES), even_ref[0], jnp.int32) == 1
    for h in range(HALVES):
        def sides(a, b):
            a, b = a.astype(f32), b.astype(f32)
            return jnp.where(even, b, a), jnp.where(even, a, b)

        if flat:
            b, r0 = sides(first_a[0, h], first_b[0, h])
            a, r1 = sides(second_a[0, h], second_b[0, h])
            o0 = own[0, 0, h]
            o1 = own[1, 0, h]
            u0 = T2 * (a + r0) + T1 * (b + o1) + T0 * o0
            u1 = T2 * (b + r1) + T1 * (o0 + r0) + T0 * o1
            partial[0, 0, h] = cz * (u1 - (T2 * o1 + T1 * (a + o0) + T0 * b))
            partial[1, 0, h] = cz * ((T2 * o0 + T1 * (o1 + r1) + T0 * r0) - u0)
            values = (cu * u0, cu * u1)
        else:
            l2, r2 = sides(far_a[0, h], far_b[0, h])
            values = (partial[0, 0, h] - (cz * T2) * l2, partial[1, 0, h] + (cz * T2) * r2)
        for i, v in enumerate(values):
            around = jnp.where(col < 8, pltpu.roll(v, COLS - 1, 0), pltpu.roll(v, 1, 0))
            for part, value in ((0, v), (1, around)):
                for level, piece in enumerate(split(value)):
                    x_s[level, i, h * COLS:(h + 1) * COLS, part * LANES:(part + 1) * LANES] = piece
    for i, plane in enumerate(planes):
        table = taps[:, :2 * LANES] if plane < 2 else taps[:, :LANES]
        out = jnp.dot(x_s[0, i], table, preferred_element_type=f32) + jnp.dot(
            x_s[1, i], table, preferred_element_type=f32
        )
        if plane < 2:
            y_s[outs.index(plane)] = out[:, :LANES]
            y_s[outs.index(2 + plane)] = out[:, LANES:]
        else:
            y_s[outs.index(2 + plane)] = out
    for i, p in enumerate(outs):
        pieces = [split(y_s[i, h * COLS:(h + 1) * COLS]) for h in range(HALVES)]
        for h in range(HALVES):
            rows = slice(h * COLS, (h + 1) * COLS)
            for level in range(2):
                w_s[level, i, rows, :LANES] = pieces[h][level]
                w_s[level, i, rows, LANES:] = jnp.where(
                    lower, pieces[(h + 1) % HALVES][level], pieces[(h - 1) % HALVES][level]
                )
        table = taps[:, 3 * LANES:] if p < 2 else taps[:, 2 * LANES:3 * LANES]
        out = jnp.dot(w_s[0, i], table, preferred_element_type=f32) + jnp.dot(
            w_s[1, i], table, preferred_element_type=f32
        )
        for h in range(HALVES):
            g_s[h, pl.ds((k * rows_of + i) * WIDE, COLS)] = out[h * COLS:(h + 1) * COLS]

    if count > rows_of * SPECIES:
        @pl.when(k == 0)
        def _():
            g_s[:, rows_of * SPECIES * WIDE:] = jnp.zeros(
                (HALVES, (count - rows_of * SPECIES) * WIDE, LANES), f32
            )

    @pl.when(k == SPECIES - 1)
    def _():
        def one_row(r, carry):
            for q in range(COLS):
                for h in range(2):
                    value = g_s[2 * r + h, pl.ds(q, count, stride=WIDE)]
                    top = value.astype(bf16).astype(f32)
                    ready[r * COLS + q, :, h * LANES:(h + 1) * LANES] = jnp.concatenate(
                        [top, value - top], axis=0
                    ).astype(bf16)
            return carry

        lax.fori_loop(0, ROWS, one_row, 0)


FLAT = (0, 1)
SLOPES = (2, 3)
ROWS_OF = {FLAT: (4, 24), SLOPES: (2, 16)}


def smooth(planes, even, taps, *planes_in):
    _, count = ROWS_OF[planes]
    half = (HALVES, COLS, LANES)
    outs = 4 if planes == FLAT else 2
    two = pl.BlockSpec((2, 1) + half, lambda k: (0, k, 0, 0, 0))
    one = pl.BlockSpec((1,) + half, lambda k: (k, 0, 0, 0))
    ready_spec = pl.BlockSpec((ROWS * COLS, 2 * count, 2 * LANES), lambda k: (0, 0, 0))
    ready_shape = jax.ShapeDtypeStruct((ROWS * COLS, 2 * count, 2 * LANES), bf16)
    partial_shape = jax.ShapeDtypeStruct((2, SPECIES) + half, f32)
    return pl.pallas_call(
        functools.partial(smooth_kernel, planes),
        name="smooth",
        grid=(SPECIES,),
        in_specs=[
            pl.BlockSpec(memory_space=SM),
            pl.BlockSpec((2 * LANES, 4 * LANES), lambda k: (0, 0)),
        ]
        + ([two, one, one, one, one] if planes == FLAT else [two, one, one]),
        out_specs=[ready_spec, two] if planes == FLAT else ready_spec,
        out_shape=[ready_shape, partial_shape] if planes == FLAT else ready_shape,
        scratch_shapes=[
            pltpu.VMEM((2, len(planes), HALVES * COLS, 2 * LANES), bf16),
            pltpu.VMEM((outs, HALVES * COLS, LANES), f32),
            pltpu.VMEM((2, outs, HALVES * COLS, 2 * LANES), bf16),
            pltpu.VMEM((HALVES, count * WIDE, LANES), f32),
        ],
        compiler_params=pltpu.CompilerParams(vmem_limit_bytes=24 * MIB),
        cost_estimate=pl.CostEstimate(flops=10**9, bytes_accessed=4 * 10**6, transcendentals=0),
    )(even, taps, *planes_in)


def row_of(k, p):
    return k * 4 + p if p < 4 else 24 + k * 2 + p - 4


def pick_kernel(cells, flat, slopes, mixed, forces, got_s):
    def one_group(g, slot):
        first = pl.multiple_of(g * GROUP, GROUP)
        for b in range(GROUP):
            d = first + b
            table = table_of(*digits_of(cells[pl.ds(d, 1), :]), 16)
            rows = jnp.concatenate([flat[d], slopes[d]], axis=0)
            got = jnp.dot(rows, table, preferred_element_type=f32)
            got = jnp.concatenate([got[:24] + got[24:48], got[48:64] + got[64:]], axis=0)
            for t in range(4):
                got_s[slot, t, pl.ds(b, 40, stride=SLOT)] = got[:, t * LANES:(t + 1) * LANES]
        for t in range(4):
            lanes = slice(t * LANES, (t + 1) * LANES)
            upper = (cells[pl.ds(first, GROUP), lanes] & 1) == 1
            vs = [mixed[k, pl.ds(first, GROUP), lanes] for k in range(SPECIES)]
            for a in range(3):
                total = None
                for k in range(SPECIES):
                    low, high = (
                        got_s[slot, t, pl.ds(row_of(k, 2 * a + z) * SLOT, GROUP)] for z in range(2)
                    )
                    value = jnp.where(upper, high, low)
                    total = vs[k] * value if total is None else total + vs[k] * value
                forces[a, pl.ds(first, GROUP), lanes] = total

    def four_groups(i, carry):
        for j in range(4):
            one_group(4 * i + j, j)
        return carry

    lax.fori_loop(0, ROWS * COLS // GROUP // 4, four_groups, 0)


def pick(cells, ready, mixed):
    return pl.pallas_call(
        pick_kernel,
        name="pick",
        in_specs=[pl.BlockSpec(memory_space=VM)] * 4,
        out_specs=pl.BlockSpec(memory_space=VM),
        out_shape=jax.ShapeDtypeStruct((3, ROWS * COLS, SLOTS), f32),
        scratch_shapes=[pltpu.VMEM((4, 4, 40 * SLOT, LANES), f32)],
        compiler_params=pltpu.CompilerParams(vmem_limit_bytes=24 * MIB),
        cost_estimate=pl.CostEstimate(flops=6 * 10**9, bytes_accessed=10**7, transcendentals=0),
    )(cells, *ready, mixed)


def body(send_cells, send_species, send_mix, send_counts, chi):
    axes = ("row", "col")
    count = lax.axis_size("row") * lax.axis_size("col")
    swap_a = [(i, i ^ 1) for i in range(count)]
    swap_b = [(i, (i + (1 if i % 2 else -1)) % count) for i in range(count)]
    odd = lax.axis_index("col") % 2
    even = (1 - odd).reshape(1)
    chis = 0.5 * (chi + chi.T) * (1.0 - jnp.eye(SPECIES, dtype=f32))
    mix_matrix = -0.5 * (chis + 1.0)
    cells, species, mix, counts = send_cells[0], send_species[0], send_mix[0], send_counts[0]
    own, first, second = deposit(counts, cells, species, mix)
    own = pltpu.with_memory_space_constraint(own, FAR)
    taps = tap_matrices()

    def swap(value, pairs):
        return lax.ppermute(value, axes, pairs)

    first_a = swap(first, swap_a)
    first_b = swap(second, swap_b)
    second_a = swap(second, swap_a)
    second_b = swap(first, swap_b)
    far_b = swap(first_a, swap_b)
    far_a = swap(first_b, swap_a)
    flat, partial = smooth(FLAT, even, taps, own, first_a, first_b, second_a, second_b)
    slopes = smooth(SLOPES, even, taps, partial, far_a, far_b)
    mixed = mixing(counts, mix_matrix, species, mix)
    return pick(cells, (flat, slopes), mixed)[None]


def solution(mesh):
    return jax.shard_map(
        body,
        mesh=mesh,
        in_specs=(
            P(("row", "col"), None, None),
            P(("row", "col"), None, None),
            P(("row", "col"), None, None, None),
            P(("row", "col"), None),
            P(),
        ),
        out_specs=P(("row", "col"), None, None, None),
        check_vma=False,
    )
```

profile of v0, /device:TPU:1, one launch (start us, length us, event | category | flops | bytes accessed | tf_op | source)
XLA Modules:
  0.0 58.3 jit_solution(17347242175053919466)
XLA Ops:
  0.0 0.0 copy-start.5
  0.0 0.0 copy-start.1
  0.0 0.0 copy-start.2
  0.0 0.0 copy-start.4
  0.0 9.2 %deposit.1 = (f32[2,6,16,16,128]{4,3,2,1,0:T(8,128)}, bf16[6,16,16,128]{3,2,1,0:T(8,128)(2,1)}, bf16[6,16,16,128]{3,2,1,0:T(8,128)(2,1)}) custom-call(s32[128]{0:T(128)} %bitcast.22, s32[128,512]{1,0:T(8,128)} %bitcast.20, s32[128,512]{1,0:T(8,128)} %bitcast.18, bf16[6,128,512]{2,1,0:T(8,128)(2,1)} %bitcast.16), custom_call_target="tpu_custom_call" | custom-call | flops 1000000000 | bytes 5000000 | tf_op jit(solution)/shard_map/deposit/pallas_call | solution.py:148
  9.2 7.7 %collective-permute-start.1 = (bf16[6,16,16,128]{3,2,1,0:T(8,128)(2,1)}, bf16[6,16,16,128]{3,2,1,0:T(8,128)(2,1)S(1)}, u32[]{:S(2)}, u32[]{:S(2)}) collective-permute-start(bf16[6,16,16,128]{3,2,1,0:T(8,128)(2,1)} %get-tuple-element.12), channel_id=1, source_target_pairs={{0,127},{1,2},{2,1},{3,4},{4,3},{5,6},{6,5},{7,8},{8,7},{9,10},{10... | collective-permute-start | bytes 1179656 | tf_op jit(solution)/shard_map/ppermute | solution.py:427
  16.9 0.0 collective-permute-start
  16.9 1.5 %collective-permute-start.2 = (bf16[6,16,16,128]{3,2,1,0:T(8,128)(2,1)}, bf16[6,16,16,128]{3,2,1,0:T(8,128)(2,1)S(1)}, u32[]{:S(2)}, u32[]{:S(2)}) collective-permute-start(bf16[6,16,16,128]{3,2,1,0:T(8,128)(2,1)} %get-tuple-element.12), channel_id=1, source_target_pairs={{0,1},{1,0},{2,3},{3,2},{4,5},{5,4},{6,7},{7,6},{8,9},{9,8},{10,11... | collective-permute-start | bytes 1179656 | tf_op jit(solution)/shard_map/ppermute | solution.py:427
  18.4 0.7 %collective-permute-start.3 = (bf16[6,16,16,128]{3,2,1,0:T(8,128)(2,1)}, bf16[6,16,16,128]{3,2,1,0:T(8,128)(2,1)S(1)}, u32[]{:S(2)}, u32[]{:S(2)}) collective-permute-start(bf16[6,16,16,128]{3,2,1,0:T(8,128)(2,1)} %get-tuple-element.11), channel_id=1, source_target_pairs={{0,127},{1,2},{2,1},{3,4},{4,3},{5,6},{6,5},{7,8},{8,7},{9,10},{10... | collective-permute-start | bytes 1179656 | tf_op jit(solution)/shard_map/ppermute | solution.py:427
  19.0 0.0 copy-done.5
  19.0 0.1 copy.7
  19.1 11.2 %collective-permute-done.1.refs_2_ = bf16[6,16,16,128]{3,2,1,0:T(8,128)(2,1)S(1)} collective-permute-done((bf16[6,16,16,128]{3,2,1,0:T(8,128)(2,1)}, bf16[6,16,16,128]{3,2,1,0:T(8,128)(2,1)S(1)}, u32[]{:S(2)}, u32[]{:S(2)}) %collective-permute-start.1) | collective-permute-done | bytes 393248 | tf_op jit(solution)/shard_map/ppermute | solution.py:427
  30.4 0.0 collective-permute-start.4
  30.4 0.0 collective-permute-done.refs_1_
  30.4 5.7 %collective-permute-start.5 = (bf16[6,16,16,128]{3,2,1,0:T(8,128)(2,1)S(1)}, bf16[6,16,16,128]{3,2,1,0:T(8,128)(2,1)S(1)}, u32[]{:S(2)}, u32[]{:S(2)}) collective-permute-start(bf16[6,16,16,128]{3,2,1,0:T(8,128)(2,1)S(1)} %collective-permute-done.refs_1_), channel_id=1, source_target_pairs={{0,127},{1,2},{2,1},{3,4},{4,3},{5,6},{6,5},{7,8},{8,7},{9,10},{10... | collective-permute-start | bytes 1179656 | tf_op jit(solution)/shard_map/ppermute | solution.py:427
  36.1 0.0 copy-done.1
  36.1 0.0 copy-done.2
  36.1 0.0 copy-done.4
  36.1 0.0 copy-start
  36.1 1.7 %mixing.1.mixed = f32[6,128,512]{2,1,0:T(8,128)S(1)} custom-call(s32[128]{0:T(128)S(1)} %bitcast.23, f32[6,6]{1,0:T(8,128)S(1)} %fusion.3.mix_matrix, s32[128,512]{1,0:T(8,128)S(1)} %bitcast.19, bf16[6,128,512]{2,1,0:T(8,128)(2,1)S(1)} %bitcast.17), custom_call_target="tpu_custom_call" | custom-call | flops 1000000000 | bytes 4000000 | tf_op jit(solution)/shard_map/mixing/pallas_call | solution.py:192
  37.8 0.0 collective-permute-done.2.refs_3_
  37.8 1.0 %collective-permute-done.3.refs_4_ = bf16[6,16,16,128]{3,2,1,0:T(8,128)(2,1)S(1)} collective-permute-done((bf16[6,16,16,128]{3,2,1,0:T(8,128)(2,1)}, bf16[6,16,16,128]{3,2,1,0:T(8,128)(2,1)S(1)}, u32[]{:S(2)}, u32[]{:S(2)}) %collective-permute-start.3) | collective-permute-done | bytes 393248 | tf_op jit(solution)/shard_map/ppermute | solution.py:427
  38.8 0.0 copy-done
  38.8 8.0 %smooth.2 = (bf16[128,48,256]{2,1,0:T(8,128)(2,1)S(1)}, f32[2,6,16,16,128]{4,3,2,1,0:T(8,128)S(1)}) custom-call(s32[1]{0:T(128)} %bitcast.1.even_ref, bf16[256,512]{1,0:T(8,128)(2,1)S(1)} %copy-done, f32[2,6,16,16,128]{4,3,2,1,0:T(8,128)} %get-tuple-element.10.refs_0_, bf16[6,16,16,128]{3,2,1,0:T(8,128)(2,1)S(1)} %collective-permute-done.refs_1_, ...), custom_call_target="tpu_custom_call" | custom-call | flops 1000000000 | bytes 4000000 | tf_op jit(solution)/shard_map/smooth/pallas_call | solution.py:340
  46.8 0.0 collective-permute-done.4.refs_1_
  46.8 0.0 collective-permute-done.5.refs_2_
  46.8 0.0 copy-start.3
  46.8 4.3 %smooth.3.slopes = bf16[128,32,256]{2,1,0:T(8,128)(2,1)S(1)} custom-call(s32[1]{0:T(128)} %bitcast.1.even_ref, bf16[256,512]{1,0:T(8,128)(2,1)S(1)} %copy-done, f32[2,6,16,16,128]{4,3,2,1,0:T(8,128)S(1)} %get-tuple-element.14.refs_0_, bf16[6,16,16,128]{3,2,1,0:T(8,128)(2,1)S(1)} %collective-permute-done.4.refs_1_, ...), custom_call_target="tpu_custom_call" | custom-call | flops 1000000000 | bytes 4000000 | tf_op jit(solution)/shard_map/smooth/pallas_call | solution.py:340
  51.1 0.0 copy-done.3
  51.2 7.1 %pick.1 = f32[3,128,512]{2,1,0:T(8,128)} custom-call(s32[128,512]{1,0:T(8,128)S(1)} %bitcast.21, bf16[128,48,256]{2,1,0:T(8,128)(2,1)S(1)} %get-tuple-element.13.flat, bf16[128,32,256]{2,1,0:T(8,128)(2,1)S(1)} %smooth.3.slopes, f32[6,128,512]{2,1,0:T(8,128)S(1)} %mixing.1.mixed), custom_call_target="tpu_custom_call" | custom-call | flops 6000000000 | bytes 10000000 | tf_op jit(solution)/shard_map/pick/pallas_call | solution.py:400
  (1 shorter events, 0.0 us)
Async XLA Ops:
  0.0 19.0 %copy-start.5 = (f32[6,6]{1,0:T(8,128)S(1)}, f32[6,6]{1,0:T(8,128)}, u32[]{:S(2)}) copy-start(f32[6,6]{1,0:T(8,128)} %param.10) | copy-start | bytes 436
  0.0 36.1 %copy-start.1 = (bf16[1,6,128,512]{3,2,1,0:T(8,128)(2,1)S(1)}, bf16[1,6,128,512]{3,2,1,0:T(8,128)(2,1)}, u32[]{:S(2)}) copy-start(bf16[1,6,128,512]{3,2,1,0:T(8,128)(2,1)} %param.8) | copy-start | bytes 2359300
  0.0 36.1 %copy-start.2 = (s32[1,128,512]{2,1,0:T(8,128)S(1)}, s32[1,128,512]{2,1,0:T(8,128)}, u32[]{:S(2)}) copy-start(s32[1,128,512]{2,1,0:T(8,128)} %param.7) | copy-start | bytes 786436
  0.0 36.1 %copy-start.4 = (s32[1,128]{1,0:T(1,128)S(1)}, s32[1,128]{1,0:T(1,128)}, u32[]{:S(2)}) copy-start(s32[1,128]{1,0:T(1,128)} %param.9) | copy-start | bytes 1540
  9.2 21.1 %collective-permute-start.1 = (bf16[6,16,16,128]{3,2,1,0:T(8,128)(2,1)}, bf16[6,16,16,128]{3,2,1,0:T(8,128)(2,1)S(1)}, u32[]{:S(2)}, u32[]{:S(2)}) collective-permute-start(bf16[6,16,16,128]{3,2,1,0:T(8,128)(2,1)} %get-tuple-element.12), channel_id=1, source_target_pairs={{0,127},{1,2},{2,1},{3,4},{4,3},{5,6},{6,5},{7,8},{8,7},{9,10},{10... | collective-permute-start | bytes 1179656 | tf_op jit(solution)/shard_map/ppermute | solution.py:427
  16.9 13.5 %collective-permute-start = (bf16[6,16,16,128]{3,2,1,0:T(8,128)(2,1)}, bf16[6,16,16,128]{3,2,1,0:T(8,128)(2,1)S(1)}, u32[]{:S(2)}, u32[]{:S(2)}) collective-permute-start(bf16[6,16,16,128]{3,2,1,0:T(8,128)(2,1)} %get-tuple-element.11), channel_id=1, source_target_pairs={{0,1},{1,0},{2,3},{3,2},{4,5},{5,4},{6,7},{7,6},{8,9},{9,8},{10,11... | collective-permute-start | bytes 1179656 | tf_op jit(solution)/shard_map/ppermute | solution.py:427
  16.9 20.9 %collective-permute-start.2 = (bf16[6,16,16,128]{3,2,1,0:T(8,128)(2,1)}, bf16[6,16,16,128]{3,2,1,0:T(8,128)(2,1)S(1)}, u32[]{:S(2)}, u32[]{:S(2)}) collective-permute-start(bf16[6,16,16,128]{3,2,1,0:T(8,128)(2,1)} %get-tuple-element.12), channel_id=1, source_target_pairs={{0,1},{1,0},{2,3},{3,2},{4,5},{5,4},{6,7},{7,6},{8,9},{9,8},{10,11... | collective-permute-start | bytes 1179656 | tf_op jit(solution)/shard_map/ppermute | solution.py:427
  18.4 20.4 %collective-permute-start.3 = (bf16[6,16,16,128]{3,2,1,0:T(8,128)(2,1)}, bf16[6,16,16,128]{3,2,1,0:T(8,128)(2,1)S(1)}, u32[]{:S(2)}, u32[]{:S(2)}) collective-permute-start(bf16[6,16,16,128]{3,2,1,0:T(8,128)(2,1)} %get-tuple-element.11), channel_id=1, source_target_pairs={{0,127},{1,2},{2,1},{3,4},{4,3},{5,6},{6,5},{7,8},{8,7},{9,10},{10... | collective-permute-start | bytes 1179656 | tf_op jit(solution)/shard_map/ppermute | solution.py:427
  30.4 16.4 %collective-permute-start.4 = (bf16[6,16,16,128]{3,2,1,0:T(8,128)(2,1)S(1)}, bf16[6,16,16,128]{3,2,1,0:T(8,128)(2,1)S(1)}, u32[]{:S(2)}, u32[]{:S(2)}) collective-permute-start(bf16[6,16,16,128]{3,2,1,0:T(8,128)(2,1)S(1)} %collective-permute-done.1.refs_2_), channel_id=1, source_target_pairs={{0,1},{1,0},{2,3},{3,2},{4,5},{5,4},{6,7},{7,6},{8,9},{9,8},{10,11... | collective-permute-start | bytes 1179656 | tf_op jit(solution)/shard_map/ppermute | solution.py:427
  30.4 16.4 %collective-permute-start.5 = (bf16[6,16,16,128]{3,2,1,0:T(8,128)(2,1)S(1)}, bf16[6,16,16,128]{3,2,1,0:T(8,128)(2,1)S(1)}, u32[]{:S(2)}, u32[]{:S(2)}) collective-permute-start(bf16[6,16,16,128]{3,2,1,0:T(8,128)(2,1)S(1)} %collective-permute-done.refs_1_), channel_id=1, source_target_pairs={{0,127},{1,2},{2,1},{3,4},{4,3},{5,6},{6,5},{7,8},{8,7},{9,10},{10... | collective-permute-start | bytes 1179656 | tf_op jit(solution)/shard_map/ppermute | solution.py:427
  36.1 2.7 %copy-start = (bf16[256,512]{1,0:T(8,128)(2,1)S(1)}, bf16[256,512]{1,0:T(8,128)(2,1)}, u32[]{:S(2)}) copy-start(bf16[256,512]{1,0:T(8,128)(2,1)} %constant.31.taps) | copy-start | bytes 786436
  46.8 4.3 %copy-start.3 = (s32[1,128,512]{2,1,0:T(8,128)S(1)}, s32[1,128,512]{2,1,0:T(8,128)}, u32[]{:S(2)}) copy-start(s32[1,128,512]{2,1,0:T(8,128)} %param.6) | copy-start | bytes 786436
where the time goes:
time: 58.4 us; the launch traced here: 58.3 us
  Pallas kernels  30.4 us (52%)
  starting transfers between devices  15.5 us (27%)
  waiting for transfers between devices  12.2 us (21%)
    ppermute x6, starting transfers between devices, swap(): return lax.ppermute(value, axes, pairs)  15.5 us
    pallas_call x2, Pallas kernels, smooth(): pl.pallas_call(functools.partial(smooth_kernel, planes), name='smooth', g...  12.3 us
    ppermute x6, waiting for transfers between devices, swap(): return lax.ppermute(value, axes, pairs)  12.2 us
    pallas_call x1, Pallas kernels, deposit(): pl.pallas_call(deposit_kernel, name='deposit', in_specs=[pl.BlockSpec(mem...  9.21 us
    pallas_call x1, Pallas kernels, pick(): pl.pallas_call(pick_kernel, name='pick', in_specs=[pl.BlockSpec(memory_sp...  7.15 us
    pallas_call x1, Pallas kernels, mixing(): pl.pallas_call(mixing_kernel, name='mixing', in_specs=[pl.BlockSpec(memor...  1.7 us
  transfers between devices with their start and end apart: 6, of which 2 were waited for; matrix products, arithmetic and copies ran while one was open for 0% of the time, Pallas kernels for 17%

commit v1 on v0

--- a/solution.py
+++ b/solution.py
@@ -363,7 +363,11 @@
     return k * 4 + p if p < 4 else 24 + k * 2 + p - 4
 
 
-def pick_kernel(cells, flat, slopes, mixed, forces, got_s):
+def pick_kernel(cells, flat, slopes, mixed, forces_far, got_s, forces, sems):
+    def result(i):
+        rows = pl.ds(pl.multiple_of(i * 4 * GROUP, 4 * GROUP), 4 * GROUP)
+        return pltpu.make_async_copy(forces.at[:, rows], forces_far.at[:, rows], sems.at[i])
+
     def one_group(g, slot):
         first = pl.multiple_of(g * GROUP, GROUP)
         for b in range(GROUP):
@@ -391,9 +395,12 @@
     def four_groups(i, carry):
         for j in range(4):
             one_group(4 * i + j, j)
+        result(i).start()
         return carry
 
     lax.fori_loop(0, ROWS * COLS // GROUP // 4, four_groups, 0)
+    for i in range(ROWS * COLS // GROUP // 4):
+        result(i).wait()
 
 
 def pick(cells, ready, mixed):
@@ -401,9 +408,13 @@
         pick_kernel,
         name="pick",
         in_specs=[pl.BlockSpec(memory_space=VM)] * 4,
-        out_specs=pl.BlockSpec(memory_space=VM),
+        out_specs=pl.BlockSpec(memory_space=FAR),
         out_shape=jax.ShapeDtypeStruct((3, ROWS * COLS, SLOTS), f32),
-        scratch_shapes=[pltpu.VMEM((4, 4, 40 * SLOT, LANES), f32)],
+        scratch_shapes=[
+            pltpu.VMEM((4, 4, 40 * SLOT, LANES), f32),
+            pltpu.VMEM((3, ROWS * COLS, SLOTS), f32),
+            pltpu.SemaphoreType.DMA((ROWS * COLS // GROUP // 4,)),
+        ],
         compiler_params=pltpu.CompilerParams(vmem_limit_bytes=24 * MIB),
         cost_estimate=pl.CostEstimate(flops=6 * 10**9, bytes_accessed=10**7, transcendentals=0),
     )(cells, *ready, mixed)

time: 58.4 us -> 58.2 us (level)
  no operation moved by 1% of the time
where the time goes in v1:
time: 58.2 us; the launch traced here: 58.1 us
  Pallas kernels  30.2 us (52%)
  starting transfers between devices  15.5 us (27%)
  waiting for transfers between devices  12.2 us (21%)
    ppermute x6, starting transfers between devices, swap(): return lax.ppermute(value, axes, pairs)  15.5 us
    pallas_call x2, Pallas kernels, smooth(): pl.pallas_call(functools.partial(smooth_kernel, planes), name='smooth', g...  12.3 us
    ppermute x6, waiting for transfers between devices, swap(): return lax.ppermute(value, axes, pairs)  12.2 us
    pallas_call x1, Pallas kernels, deposit(): pl.pallas_call(deposit_kernel, name='deposit', in_specs=[pl.BlockSpec(mem...  9.21 us
    pallas_call x1, Pallas kernels, pick(): pl.pallas_call(pick_kernel, name='pick', in_specs=[pl.BlockSpec(memory_sp...  6.94 us
    pallas_call x1, Pallas kernels, mixing(): pl.pallas_call(mixing_kernel, name='mixing', in_specs=[pl.BlockSpec(memor...  1.7 us
  transfers between devices with their start and end apart: 6, of which 2 were waited for; matrix products, arithmetic and copies ran while one was open for 0% of the time, Pallas kernels for 17%

profile of v1, /device:TPU:1, one launch (start us, length us, event | category | flops | bytes accessed | tf_op | source)
XLA Modules:
  0.0 58.1 jit_solution(5979724402601716181)
XLA Ops:
  0.0 0.0 copy-start.5
  0.0 0.0 copy-start.1
  0.0 0.0 copy-start.2
  0.0 0.0 copy-start.4
  0.0 9.2 %deposit.1 = (f32[2,6,16,16,128]{4,3,2,1,0:T(8,128)}, bf16[6,16,16,128]{3,2,1,0:T(8,128)(2,1)}, bf16[6,16,16,128]{3,2,1,0:T(8,128)(2,1)}) custom-call(s32[128]{0:T(128)} %bitcast.22, s32[128,512]{1,0:T(8,128)} %bitcast.20, s32[128,512]{1,0:T(8,128)} %bitcast.18, bf16[6,128,512]{2,1,0:T(8,128)(2,1)} %bitcast.16), custom_call_target="tpu_custom_call" | custom-call | flops 1000000000 | bytes 5000000 | tf_op jit(solution)/shard_map/deposit/pallas_call | solution.py:148
  9.2 7.7 %collective-permute-start.1 = (bf16[6,16,16,128]{3,2,1,0:T(8,128)(2,1)}, bf16[6,16,16,128]{3,2,1,0:T(8,128)(2,1)S(1)}, u32[]{:S(2)}, u32[]{:S(2)}) collective-permute-start(bf16[6,16,16,128]{3,2,1,0:T(8,128)(2,1)} %get-tuple-element.12), channel_id=1, source_target_pairs={{0,127},{1,2},{2,1},{3,4},{4,3},{5,6},{6,5},{7,8},{8,7},{9,10},{10... | collective-permute-start | bytes 1179656 | tf_op jit(solution)/shard_map/ppermute | solution.py:438
  16.9 0.0 collective-permute-start
  16.9 1.5 %collective-permute-start.2 = (bf16[6,16,16,128]{3,2,1,0:T(8,128)(2,1)}, bf16[6,16,16,128]{3,2,1,0:T(8,128)(2,1)S(1)}, u32[]{:S(2)}, u32[]{:S(2)}) collective-permute-start(bf16[6,16,16,128]{3,2,1,0:T(8,128)(2,1)} %get-tuple-element.12), channel_id=1, source_target_pairs={{0,1},{1,0},{2,3},{3,2},{4,5},{5,4},{6,7},{7,6},{8,9},{9,8},{10,11... | collective-permute-start | bytes 1179656 | tf_op jit(solution)/shard_map/ppermute | solution.py:438
  18.4 0.7 %collective-permute-start.3 = (bf16[6,16,16,128]{3,2,1,0:T(8,128)(2,1)}, bf16[6,16,16,128]{3,2,1,0:T(8,128)(2,1)S(1)}, u32[]{:S(2)}, u32[]{:S(2)}) collective-permute-start(bf16[6,16,16,128]{3,2,1,0:T(8,128)(2,1)} %get-tuple-element.11), channel_id=1, source_target_pairs={{0,127},{1,2},{2,1},{3,4},{4,3},{5,6},{6,5},{7,8},{8,7},{9,10},{10... | collective-permute-start | bytes 1179656 | tf_op jit(solution)/shard_map/ppermute | solution.py:438
  19.0 0.0 copy-done.5
  19.0 0.1 copy.7
  19.1 11.2 %collective-permute-done.1.refs_2_ = bf16[6,16,16,128]{3,2,1,0:T(8,128)(2,1)S(1)} collective-permute-done((bf16[6,16,16,128]{3,2,1,0:T(8,128)(2,1)}, bf16[6,16,16,128]{3,2,1,0:T(8,128)(2,1)S(1)}, u32[]{:S(2)}, u32[]{:S(2)}) %collective-permute-start.1) | collective-permute-done | bytes 393248 | tf_op jit(solution)/shard_map/ppermute | solution.py:438
  30.4 0.0 collective-permute-start.4
  30.4 0.0 collective-permute-done.refs_1_
  30.4 5.7 %collective-permute-start.5 = (bf16[6,16,16,128]{3,2,1,0:T(8,128)(2,1)S(1)}, bf16[6,16,16,128]{3,2,1,0:T(8,128)(2,1)S(1)}, u32[]{:S(2)}, u32[]{:S(2)}) collective-permute-start(bf16[6,16,16,128]{3,2,1,0:T(8,128)(2,1)S(1)} %collective-permute-done.refs_1_), channel_id=1, source_target_pairs={{0,127},{1,2},{2,1},{3,4},{4,3},{5,6},{6,5},{7,8},{8,7},{9,10},{10... | collective-permute-start | bytes 1179656 | tf_op jit(solution)/shard_map/ppermute | solution.py:438
  36.1 0.0 copy-done.1
  36.1 0.0 copy-done.2
  36.1 0.0 copy-done.4
  36.1 0.0 copy-start
  36.1 1.7 %mixing.1.mixed = f32[6,128,512]{2,1,0:T(8,128)S(1)} custom-call(s32[128]{0:T(128)S(1)} %bitcast.23, f32[6,6]{1,0:T(8,128)S(1)} %fusion.3.mix_matrix, s32[128,512]{1,0:T(8,128)S(1)} %bitcast.19, bf16[6,128,512]{2,1,0:T(8,128)(2,1)S(1)} %bitcast.17), custom_call_target="tpu_custom_call" | custom-call | flops 1000000000 | bytes 4000000 | tf_op jit(solution)/shard_map/mixing/pallas_call | solution.py:192
  37.8 0.0 collective-permute-done.2.refs_3_
  37.8 1.0 %collective-permute-done.3.refs_4_ = bf16[6,16,16,128]{3,2,1,0:T(8,128)(2,1)S(1)} collective-permute-done((bf16[6,16,16,128]{3,2,1,0:T(8,128)(2,1)}, bf16[6,16,16,128]{3,2,1,0:T(8,128)(2,1)S(1)}, u32[]{:S(2)}, u32[]{:S(2)}) %collective-permute-start.3) | collective-permute-done | bytes 393248 | tf_op jit(solution)/shard_map/ppermute | solution.py:438
  38.8 0.0 copy-done
  38.8 8.0 %smooth.2 = (bf16[128,48,256]{2,1,0:T(8,128)(2,1)S(1)}, f32[2,6,16,16,128]{4,3,2,1,0:T(8,128)S(1)}) custom-call(s32[1]{0:T(128)} %bitcast.1.even_ref, bf16[256,512]{1,0:T(8,128)(2,1)S(1)} %copy-done, f32[2,6,16,16,128]{4,3,2,1,0:T(8,128)} %get-tuple-element.10.refs_0_, bf16[6,16,16,128]{3,2,1,0:T(8,128)(2,1)S(1)} %collective-permute-done.refs_1_, ...), custom_call_target="tpu_custom_call" | custom-call | flops 1000000000 | bytes 4000000 | tf_op jit(solution)/shard_map/smooth/pallas_call | solution.py:340
  46.8 0.0 collective-permute-done.4.refs_1_
  46.8 0.0 collective-permute-done.5.refs_2_
  46.8 0.0 copy-start.3
  46.8 4.3 %smooth.3.slopes = bf16[128,32,256]{2,1,0:T(8,128)(2,1)S(1)} custom-call(s32[1]{0:T(128)} %bitcast.1.even_ref, bf16[256,512]{1,0:T(8,128)(2,1)S(1)} %copy-done, f32[2,6,16,16,128]{4,3,2,1,0:T(8,128)S(1)} %get-tuple-element.14.refs_0_, bf16[6,16,16,128]{3,2,1,0:T(8,128)(2,1)S(1)} %collective-permute-done.4.refs_1_, ...), custom_call_target="tpu_custom_call" | custom-call | flops 1000000000 | bytes 4000000 | tf_op jit(solution)/shard_map/smooth/pallas_call | solution.py:340
  51.1 0.0 copy-done.3
  51.2 6.9 %pick.1 = f32[3,128,512]{2,1,0:T(8,128)} custom-call(s32[128,512]{1,0:T(8,128)S(1)} %bitcast.21, bf16[128,48,256]{2,1,0:T(8,128)(2,1)S(1)} %get-tuple-element.13.flat, bf16[128,32,256]{2,1,0:T(8,128)(2,1)S(1)} %smooth.3.slopes, f32[6,128,512]{2,1,0:T(8,128)S(1)} %mixing.1.mixed), custom_call_target="tpu_custom_call" | custom-call | flops 6000000000 | bytes 10000000 | tf_op jit(solution)/shard_map/pick/pallas_call | solution.py:407
  (1 shorter events, 0.0 us)
Async XLA Ops:
  0.0 19.0 %copy-start.5 = (f32[6,6]{1,0:T(8,128)S(1)}, f32[6,6]{1,0:T(8,128)}, u32[]{:S(2)}) copy-start(f32[6,6]{1,0:T(8,128)} %param.10) | copy-start | bytes 436
  0.0 36.1 %copy-start.1 = (bf16[1,6,128,512]{3,2,1,0:T(8,128)(2,1)S(1)}, bf16[1,6,128,512]{3,2,1,0:T(8,128)(2,1)}, u32[]{:S(2)}) copy-start(bf16[1,6,128,512]{3,2,1,0:T(8,128)(2,1)} %param.8) | copy-start | bytes 2359300
  0.0 36.1 %copy-start.2 = (s32[1,128,512]{2,1,0:T(8,128)S(1)}, s32[1,128,512]{2,1,0:T(8,128)}, u32[]{:S(2)}) copy-start(s32[1,128,512]{2,1,0:T(8,128)} %param.7) | copy-start | bytes 786436
  0.0 36.1 %copy-start.4 = (s32[1,128]{1,0:T(1,128)S(1)}, s32[1,128]{1,0:T(1,128)}, u32[]{:S(2)}) copy-start(s32[1,128]{1,0:T(1,128)} %param.9) | copy-start | bytes 1540
  9.2 21.1 %collective-permute-start.1 = (bf16[6,16,16,128]{3,2,1,0:T(8,128)(2,1)}, bf16[6,16,16,128]{3,2,1,0:T(8,128)(2,1)S(1)}, u32[]{:S(2)}, u32[]{:S(2)}) collective-permute-start(bf16[6,16,16,128]{3,2,1,0:T(8,128)(2,1)} %get-tuple-element.12), channel_id=1, source_target_pairs={{0,127},{1,2},{2,1},{3,4},{4,3},{5,6},{6,5},{7,8},{8,7},{9,10},{10... | collective-permute-start | bytes 1179656 | tf_op jit(solution)/shard_map/ppermute | solution.py:438
  16.9 13.5 %collective-permute-start = (bf16[6,16,16,128]{3,2,1,0:T(8,128)(2,1)}, bf16[6,16,16,128]{3,2,1,0:T(8,128)(2,1)S(1)}, u32[]{:S(2)}, u32[]{:S(2)}) collective-permute-start(bf16[6,16,16,128]{3,2,1,0:T(8,128)(2,1)} %get-tuple-element.11), channel_id=1, source_target_pairs={{0,1},{1,0},{2,3},{3,2},{4,5},{5,4},{6,7},{7,6},{8,9},{9,8},{10,11... | collective-permute-start | bytes 1179656 | tf_op jit(solution)/shard_map/ppermute | solution.py:438
  16.9 20.9 %collective-permute-start.2 = (bf16[6,16,16,128]{3,2,1,0:T(8,128)(2,1)}, bf16[6,16,16,128]{3,2,1,0:T(8,128)(2,1)S(1)}, u32[]{:S(2)}, u32[]{:S(2)}) collective-permute-start(bf16[6,16,16,128]{3,2,1,0:T(8,128)(2,1)} %get-tuple-element.12), channel_id=1, source_target_pairs={{0,1},{1,0},{2,3},{3,2},{4,5},{5,4},{6,7},{7,6},{8,9},{9,8},{10,11... | collective-permute-start | bytes 1179656 | tf_op jit(solution)/shard_map/ppermute | solution.py:438
  18.4 20.4 %collective-permute-start.3 = (bf16[6,16,16,128]{3,2,1,0:T(8,128)(2,1)}, bf16[6,16,16,128]{3,2,1,0:T(8,128)(2,1)S(1)}, u32[]{:S(2)}, u32[]{:S(2)}) collective-permute-start(bf16[6,16,16,128]{3,2,1,0:T(8,128)(2,1)} %get-tuple-element.11), channel_id=1, source_target_pairs={{0,127},{1,2},{2,1},{3,4},{4,3},{5,6},{6,5},{7,8},{8,7},{9,10},{10... | collective-permute-start | bytes 1179656 | tf_op jit(solution)/shard_map/ppermute | solution.py:438
  30.4 16.4 %collective-permute-start.4 = (bf16[6,16,16,128]{3,2,1,0:T(8,128)(2,1)S(1)}, bf16[6,16,16,128]{3,2,1,0:T(8,128)(2,1)S(1)}, u32[]{:S(2)}, u32[]{:S(2)}) collective-permute-start(bf16[6,16,16,128]{3,2,1,0:T(8,128)(2,1)S(1)} %collective-permute-done.1.refs_2_), channel_id=1, source_target_pairs={{0,1},{1,0},{2,3},{3,2},{4,5},{5,4},{6,7},{7,6},{8,9},{9,8},{10,11... | collective-permute-start | bytes 1179656 | tf_op jit(solution)/shard_map/ppermute | solution.py:438
  30.4 16.4 %collective-permute-start.5 = (bf16[6,16,16,128]{3,2,1,0:T(8,128)(2,1)S(1)}, bf16[6,16,16,128]{3,2,1,0:T(8,128)(2,1)S(1)}, u32[]{:S(2)}, u32[]{:S(2)}) collective-permute-start(bf16[6,16,16,128]{3,2,1,0:T(8,128)(2,1)S(1)} %collective-permute-done.refs_1_), channel_id=1, source_target_pairs={{0,127},{1,2},{2,1},{3,4},{4,3},{5,6},{6,5},{7,8},{8,7},{9,10},{10... | collective-permute-start | bytes 1179656 | tf_op jit(solution)/shard_map/ppermute | solution.py:438
  36.1 2.7 %copy-start = (bf16[256,512]{1,0:T(8,128)(2,1)S(1)}, bf16[256,512]{1,0:T(8,128)(2,1)}, u32[]{:S(2)}) copy-start(bf16[256,512]{1,0:T(8,128)(2,1)} %constant.31.taps) | copy-start | bytes 786436
  46.8 4.3 %copy-start.3 = (s32[1,128,512]{2,1,0:T(8,128)S(1)}, s32[1,128,512]{2,1,0:T(8,128)}, u32[]{:S(2)}) copy-start(s32[1,128,512]{2,1,0:T(8,128)} %param.6) | copy-start | bytes 786436
